TPU v7x, 256 devices: a whole 4x4x8 slice. The times are simulated.
256 devices in a mesh: row: 16 (over y, x), col: 16 (over z, core).
Axes of the slice: x: 4, y: 4, z: 8, core: 2. Of those that a mesh axis runs over, the one named last changes fastest.
Arguments:
- source: float32 [2048, 64, 128], P(('row', 'col')), may hold values from -6 to 6
- blocks: float32 [65536, 64, 64], P(('row', 'col')), may hold values from -0.15625 to 0.15625
- row_index: int32 [65536], P(('row', 'col')), may hold values from 0 to 127
- col_index: int32 [65536], P(('row', 'col')), may hold values from 0 to 127
- live_count: int32 [256], P(('row', 'col')), may hold values from 64 to 256, as said below
Outputs:
- irradiance: float32 [2048, 64, 128], P(('row', 'col'))
Inputs may be any that keep to these rules, and one draw needn't show every extreme that they name: `live_count`: slots of a device beyond its live count are padding; some device has all 256 slots live.
All inputs are finite; a program needn't handle non-finite values.
Results may differ from a plain program's by a relative error of at most 0.0003.
Values sent between devices are 32-bit elements; how exact they have to be, the bound alone decides.
A program may use at most 128 MiB of HBM per device.

v0:
```python
import jax
import jax.numpy as jnp
from jax import lax
from jax.sharding import PartitionSpec as P

ITERS = 2


def local_transfer(blocks, gathered, row_ids, col_index, group_rows):
    picked = jnp.take(gathered, col_index, axis=0)
    products = jnp.einsum("nij,njl->nil", blocks, picked, precision=lax.Precision.HIGHEST)
    summed = jax.ops.segment_sum(products, row_ids, num_segments=group_rows + 1)
    return summed[:group_rows]


def body(source, blocks, row_index, col_index, live_count):
    bricks_here = source.shape[0]
    group_rows = bricks_here * lax.axis_size("col")
    live_total = live_count[0]
    slot_ids = jnp.arange(blocks.shape[0], dtype=jnp.int32)
    row_ids = jnp.where(slot_ids < live_total, row_index, group_rows)
    field = source
    for bounce in range(ITERS):
        gathered = lax.all_gather(field, "row", axis=0, tiled=True)
        partial_value = local_transfer(blocks, gathered, row_ids, col_index, group_rows)
        whole = lax.psum(partial_value, "col")
        owned = lax.dynamic_slice_in_dim(whole, lax.axis_index("col") * bricks_here, bricks_here, 0)
        field = source + owned
    return field


def solution(mesh):
    in_specs = (
        P(("row", "col"), None, None),
        P(("row", "col"), None, None),
        P(("row", "col")),
        P(("row", "col")),
        P(("row", "col")),
    )
    out_specs = P(("row", "col"), None, None)
    return jax.shard_map(body, mesh=mesh, in_specs=in_specs, out_specs=out_specs, check_vma=False)
```

profile of v0, /device:TPU:1, one launch (start us, length us, event | category | flops | bytes accessed | tf_op | source)
XLA Modules:
  0.0 516.6 jit_solution(3725218833665404875)
XLA Ops:
  6.5 0.7 all-gather.3.cloned.1.call-update
  7.3 0.0 all-reduce.3.cloned.1.call-start
  7.3 9.2 %copy.7 = f32[256,64,64]{2,1,0:T(8,128)} copy(f32[256,64,64]{0,2,1:T(8,128)} %param.8) | data formatting | bytes 8388608 | tf_op args[1]
  17.2 52.7 %all-gather.3.cloned.1.call-done = f32[128,64,128]{2,1,0:T(8,128)} async-done(((f32[8,64,128]{2,1,0:T(8,128)}), f32[128,64,128]{2,1,0:T(8,128)}) %all-gather.3.cloned.1.call-update) | async-done | bytes 4194320 | tf_op jit(solution)/shard_map/all_gather | solution.py:24
  69.8 6.5 %gather_fusion = f32[256,64,128]{2,1,0:T(8,128)} fusion(f32[128,64,128]{2,1,0:T(8,128)} %all-gather.3.cloned.1.call-done, s32[1024]{0:T(1024)S(1)} %pad_clamp_fusion), kind=kCustom, calls=%fused_computation.clone | custom fusion | bytes 16778240 | tf_op jit(solution)/shard_map/jit(_take)/gather | solution.py:10
  76.3 14.7 %fusion.8 = f32[256,64,128]{2,1,0:T(8,128)} fusion(f32[256,64,64]{2,1,0:T(8,128)} %copy.7, f32[256,64,128]{2,1,0:T(8,128)} %gather_fusion, pred[256]{0:T(512)(128)(4,1)S(1)} %compare_and_fusion), kind=kOutput, calls=%fused_computation.12 | convolution fusion | flops 1612709888 | bytes 20971776 | tf_op jit(solution)/shard_map/nij,njl->nil/dot_general | solution.py:11
  91.0 2.5 broadcast.6.clone
  93.5 39.5 %scatter_fusion = f32[129,64,128]{2,1,0:T(8,128)} fusion(f32[129,64,128]{2,1,0:T(8,128)} %broadcast.6.clone, s32[256]{0:T(256)S(1)} %compare_select_fusion.1, f32[256,64,128]{2,1,0:T(8,128)} %fusion.8), kind=kCustom, calls=%fused_computation.2 | custom fusion | flops 2097152 | bytes 25166848 | tf_op jit(solution)/shard_map/scatter-add | solution.py:12
  133.0 4.8 slice.12
  137.8 0.0 all-reduce.3.cloned.1.call-update
  137.8 0.0 all-gather.5.cloned.1.call-start
  137.8 121.5 %all-reduce.3.cloned.1.call-done = f32[128,64,128]{2,1,0:T(8,128)} async-done(((f32[128,64,128]{2,1,0:T(8,128)}), f32[128,64,128]{2,1,0:T(8,128)}) %all-reduce.3.cloned.1.call-update) | async-done | bytes 4194320 | tf_op jit(solution)/shard_map/psum | solution.py:26
  259.4 1.7 dynamic-slice_add_fusion.1
  261.1 0.0 all-gather.5.cloned.1.call-update
  261.1 0.2 all-reduce.5.cloned.1.call-start
  261.3 57.4 %all-gather.5.cloned.1.call-done = f32[128,64,128]{2,1,0:T(8,128)} async-done(((f32[8,64,128]{2,1,0:T(8,128)}), f32[128,64,128]{2,1,0:T(8,128)}) %all-gather.5.cloned.1.call-update) | async-done | bytes 4194320 | tf_op jit(solution)/shard_map/all_gather | solution.py:24
  318.7 6.5 %gather_fusion.1 = f32[256,64,128]{2,1,0:T(8,128)} fusion(f32[128,64,128]{2,1,0:T(8,128)} %all-gather.5.cloned.1.call-done, s32[1024]{0:T(1024)S(1)} %pad_clamp_fusion), kind=kCustom, calls=%fused_computation.1.clone | custom fusion | bytes 16778240 | tf_op jit(solution)/shard_map/jit(_take)/gather | solution.py:10
  325.2 14.7 %fusion.11 = f32[256,64,128]{2,1,0:T(8,128)} fusion(f32[256,64,64]{2,1,0:T(8,128)} %copy.7, f32[256,64,128]{2,1,0:T(8,128)} %gather_fusion.1, pred[256]{0:T(512)(128)(4,1)S(1)} %compare_and_fusion), kind=kOutput, calls=%fused_computation.13 | convolution fusion | flops 1612709888 | bytes 20971776 | tf_op jit(solution)/shard_map/nij,njl->nil/dot_general | solution.py:11
  339.9 2.5 broadcast.6
  342.3 39.5 %scatter_fusion.1 = f32[129,64,128]{2,1,0:T(8,128)} fusion(f32[129,64,128]{2,1,0:T(8,128)} %broadcast.6, s32[256]{0:T(256)S(1)} %compare_select_fusion.1, f32[256,64,128]{2,1,0:T(8,128)} %fusion.11), kind=kCustom, calls=%fused_computation.3 | custom fusion | flops 2097152 | bytes 25166848 | tf_op jit(solution)/shard_map/scatter-add | solution.py:12
  381.8 4.8 slice.13
  386.6 0.0 all-reduce.5.cloned.1.call-update
  386.6 121.8 %all-reduce.5.cloned.1.call-done = f32[128,64,128]{2,1,0:T(8,128)} async-done(((f32[128,64,128]{2,1,0:T(8,128)}), f32[128,64,128]{2,1,0:T(8,128)}) %all-reduce.5.cloned.1.call-update) | async-done | bytes 4194320 | tf_op jit(solution)/shard_map/psum | solution.py:26
  508.4 1.7 dynamic-slice_add_fusion
  (11 shorter events, 0.0 us)
Async XLA Ops:
  6.5 10.6 %copy-start.1 = (s32[256]{0:T(256)S(1)}, s32[256]{0:T(256)}, u32[]{:S(2)}) copy-start(s32[256]{0:T(256)} %param.10) | copy-start | bytes 3076
  6.5 10.6 %copy-start.2 = (s32[256]{0:T(256)S(1)}, s32[256]{0:T(256)}, u32[]{:S(2)}) copy-start(s32[256]{0:T(256)} %param.9) | copy-start | bytes 3076
  6.5 63.3 %all-gather.3.cloned.1.call-start = ((), (), s32[]{:S(2)}) async-start(), calls=%async_computation | async-start | bytes 4456448 | tf_op jit(solution)/shard_map/all_gather | solution.py:24
  7.3 252.1 %all-reduce.3.cloned.1.call-start = ((), (), s32[]{:S(2)}) async-start(), calls=%async_computation.1 | async-start | bytes 8388608 | tf_op jit(solution)/shard_map/psum | solution.py:26
  133.0 126.4 %copy-start = (f32[8,64,128]{2,1,0:T(8,128)S(1)}, f32[8,64,128]{2,1,0:T(8,128)}, u32[]{:S(2)}) copy-start(f32[8,64,128]{2,1,0:T(8,128)} %param.7) | copy-start | bytes 786436
  137.8 180.9 %all-gather.5.cloned.1.call-start = ((), (), s32[]{:S(2)}) async-start(), calls=%async_computation.2 | async-start | bytes 4456448 | tf_op jit(solution)/shard_map/all_gather | solution.py:24
  261.1 247.3 %all-reduce.5.cloned.1.call-start = ((), (), s32[]{:S(2)}) async-start(), calls=%async_computation.3 | async-start | bytes 8388608 | tf_op jit(solution)/shard_map/psum | solution.py:26
Sparse Core Ops, SparseCore 0:
  9.8 60.0 all-gather.2
  137.9 121.4 all-reduce.2
  261.8 56.8 all-gather.4
  386.7 121.6 all-reduce.4
where the time goes:
time: 518 us; the launch traced here: 517 us
  waiting for transfers between devices  354 us (68%)
  other arithmetic  82.4 us (16%)
  local copies, waits for them, and re-layouts  36.6 us (7%)
  matrix products  29.3 us (6%)
  between operations  13.8 us (3%)
    psum x2, waiting for transfers between devices, body(): whole = lax.psum(partial_value, 'col')  243 us
    all_gather x2, waiting for transfers between devices, body(): gathered = lax.all_gather(field, 'row', axis=0, tiled=True)  110 us
    scatter-add x2, other arithmetic, local_transfer(): summed = jax.ops.segment_sum(products, row_ids, num_segments=group_rows + 1)  79 us
    dot_general x2, matrix products, local_transfer(): jnp.einsum('nij,njl->nil', blocks, picked, precision=lax.Precision.HIGHEST)  29.3 us
    gather x2, local copies, waits for them, and re-layouts, local_transfer(): picked = jnp.take(gathered, col_index, axis=0)  13 us
  transfers between devices with their start and end apart: 4, of which 4 were waited for; matrix products, arithmetic and copies ran while one was open for 2% of the time, Pallas kernels for 0%

commit v1 on v0

v1 whole, which is shorter than its diff:
```python
import jax
import jax.numpy as jnp
from jax import lax
from jax.experimental import pallas as pl
from jax.experimental.pallas import tpu as pltpu
from jax.sharding import PartitionSpec as P

MESH = pl.DeviceIdType.MESH
ITERS = 2
GROUPS = 2
TILES = 4
SLOTS = 256
ROWS = 16
ZN = 8
ZSHIFT = (4, 3, 5, 2, 6, 1, 7, 0)
UNROLL = 8
PIECES = 8
LINES = (0, 3, 1, 2)
OFF = (0, 2, 6, 10)
SPAN = 14


def rem(a, n):
    return lax.rem(a, n)


class Schedule:
    def __init__(self):
        self.tasks = []

    def add(self, when, run):
        self.tasks.append((when, len(self.tasks), run))

    def run(self):
        for _, _, run in sorted(self.tasks, key=lambda task: task[:2]):
            run()


def kernel(
    src_hbm, blk_hbm, rank_ref, mi, mf, out_ref,
    xg, xs0, xs1, a_ref, wide, c_ref, raw, perm, po, px, cx, rp, sp, fx, srcv,
    ag_s, ag_r, cx_s, cx_r, rs_s, rs_r, blk_sem, src_sem,
):
    xs = (xs0, xs1)
    row, col = lax.axis_index("row"), lax.axis_index("col")
    y, x = row // 4, rem(row, 4)
    z, h = col // 2, rem(col, 2)

    def at(i, j):
        return rem(y + i * h + j * (1 - h), 4) * 4 + rem(x + i * (1 - h) + j * h, 4)

    def zcol(d):
        return rem(z + d, ZN) * 2 + h

    partner = z * 2 + (1 - h)

    blk_copies = [
        pltpu.make_async_copy(blk_hbm.at[pl.ds(16 * n, 16)], raw.at[pl.ds(16 * n, 16)], blk_sem.at[n]) for n in range(4)
    ]
    src_copy = pltpu.make_async_copy(src_hbm, srcv, src_sem)
    src_copy.start()
    for copy in blk_copies:
        copy.start()

    barrier = pltpu.get_barrier_semaphore()
    peers = [(at(1, 0), col), (at(3, 0), col), (at(0, 1), col), (at(0, 3), col)]
    peers += [(row, zcol(1)), (row, zcol(7)), (row, partner)]
    for peer in peers:
        pl.semaphore_signal(barrier, inc=1, device_id=peer, device_id_type=MESH)

    lane = lax.broadcasted_iota(jnp.int32, (64, 128), 1)
    low = lane < 64
    half = jnp.where(lax.broadcasted_iota(jnp.int32, (8, 128), 1) < 64, 1.0, 0.0).astype(jnp.float32)
    flip = 1.0 - 2.0 * half

    src_copy.wait()
    for j in range(TILES):
        even, odd = srcv[2 * j], srcv[2 * j + 1]
        xg[row * 8 + j] = jnp.where(low, even, pltpu.roll(odd, 64, 1))
        xg[row * 8 + TILES + j] = jnp.where(low, pltpu.roll(even, 64, 1), odd)

    pl.semaphore_wait(barrier, len(peers))


    def tile0(b, g, r):
        return b * 128 + r * 8 + g * TILES

    def ag(b, g, k, r, t0, n, dest):
        ref = xg.at[pl.ds(tile0(b, g, r) + t0, n)]
        i = (b * GROUPS + g) * 20 + k
        return pltpu.make_async_remote_copy(
            src_ref=ref, dst_ref=ref, send_sem=ag_s.at[i], recv_sem=ag_r.at[i], device_id=(dest, col), device_id_type=MESH
        )

    pending = []

    def go(copy):
        copy.start()
        pending.append(copy)

    def split(b, g, r, t0=0, n=TILES):
        def one(t, carry):
            tile = xg[tile0(b, g, r) + t0 + t]
            for v, val in enumerate((tile, pltpu.roll(tile, 64, 1))):
                hi = val.astype(jnp.bfloat16)
                lo = (val - hi.astype(jnp.float32)).astype(jnp.bfloat16)
                at_ = (r * TILES + t0 + t) * 2 + v
                xs[g][at_, pl.ds(0, 64), :] = hi
                xs[g][at_, pl.ds(64, 64), :] = lo
            return carry

        lax.fori_loop(0, n, one, 0)

    def gather_own(b, g):
        go(ag(b, g, 0, row, 0, 4, at(1, 0)))
        go(ag(b, g, 1, row, 0, 4, at(3, 0)))
        go(ag(b, g, 4, row, 0, 4, at(0, 1)))
        go(ag(b, g, 5, row, 0, 4, at(0, 3)))

    def line_out(b, g, li):
        r = at(LINES[li], 0)
        go(ag(b, g, 4 + 4 * li, r, 0, 4, at(0, 1)))
        go(ag(b, g, 5 + 4 * li, r, 0, 4, at(0, 3)))

    def first_full(b, g, k):
        r = at(3, 0) if k == 0 else at(1, 0)
        ag(b, g, k, r, 0, 4, row).wait_recv()
        if k == 0:
            go(ag(b, g, 2, r, 0, 2, at(1, 0)))
        else:
            go(ag(b, g, 3, r, 2, 2, at(3, 0)))
        line_out(b, g, 1 + k)
        split(b, g, r)

    def first_far(b, g):
        r = at(2, 0)
        ag(b, g, 2, r, 0, 2, row).wait_recv()
        ag(b, g, 3, r, 2, 2, row).wait_recv()
        line_out(b, g, 3)
        split(b, g, r)

    def line_full(b, g, li, k):
        r = at(LINES[li], 3) if k == 0 else at(LINES[li], 1)
        ag(b, g, 4 + 4 * li + k, r, 0, 4, row).wait_recv()
        if k == 0:
            go(ag(b, g, 6 + 4 * li, r, 0, 2, at(0, 1)))
        else:
            go(ag(b, g, 7 + 4 * li, r, 2, 2, at(0, 3)))
        split(b, g, r)

    def line_far(b, g, li):
        r = at(LINES[li], 2)
        ag(b, g, 6 + 4 * li, r, 0, 2, row).wait_recv()
        ag(b, g, 7 + 4 * li, r, 2, 2, row).wait_recv()
        split(b, g, r)


    perm[...] = jnp.where(lax.broadcasted_iota(jnp.int32, (SLOTS, SLOTS), 0) == rank_ref[...], 1.0, 0.0).astype(jnp.bfloat16)

    def sort_blocks(part, n):
        if part == 0:
            blk_copies[n].wait()

        def one(i, carry):
            val = raw[i]
            hi = val.astype(jnp.bfloat16)
            lo = (val - hi.astype(jnp.float32)).astype(jnp.bfloat16)
            four = jnp.concatenate([hi, hi, lo, lo], axis=0)
            order = perm[pl.ds(128 * part, 128), :]
            res = lax.dot_general(order, four, (((1,), (1,)), ((), ())), preferred_element_type=jnp.float32)
            wide[pl.ds(i, 128, stride=128), :] = res[:, :128]
            wide[pl.ds(64 + i, 128, stride=128), :] = res[:, 128:]
            return carry

        lax.fori_loop(16 * n, 16 * n + 16, one, 0)

    def pack_blocks(part):
        def one(p, carry):
            a_ref[128 * part + p] = wide[pl.ds(pl.multiple_of(p * 128, 128), 128), :].astype(jnp.bfloat16)
            return carry

        lax.fori_loop(0, 128, one, 0)


    def products(g, piece):
        start = piece * (SLOTS // PIECES)

        def body(it, acc):
            base = start + it * UNROLL
            found = [
                jnp.dot(a_ref[base + u], xs[g][mi[base + u]], preferred_element_type=jnp.float32) for u in range(UNROLL)
            ]
            for u in range(UNROLL):
                p = base + u
                mask = half + mf[SLOTS + p] * flip
                both = found[u][:64] + found[u][64:]
                both = (both.reshape(8, 8, 128) * mask[None]).reshape(64, 128)
                acc = acc * mf[p] + both
                c_ref[p] = acc
            return acc

        acc = c_ref[start - 1] if piece else jnp.zeros((64, 128), jnp.float32)
        lax.fori_loop(0, SLOTS // PIECES // UNROLL, body, acc)

    def partial_sum(zc, core, t):
        q = (zc * 2 + core) * TILES + t
        return c_ref[mi[SLOTS + q]] * mf[2 * SLOTS + q]

    def cx_copy(b, g, o):
        i = (b * GROUPS + g) * ZN + o
        return pltpu.make_async_remote_copy(
            src_ref=px.at[pl.ds((g * ZN + o) * TILES, TILES)], dst_ref=cx.at[pl.ds(i * TILES, TILES)],
            send_sem=cx_s.at[i], recv_sem=cx_r.at[i], device_id=(row, partner), device_id_type=MESH,
        )

    def sums(b, g):
        if b:
            for o in range(ZN):
                cx_copy(b - 1, g, o).wait_send()
        for o in range(ZN):
            for t in range(TILES):
                px[(g * ZN + o) * TILES + t] = partial_sum(rem(z + ZSHIFT[o], ZN), 1 - h, t)
            if o:
                cx_copy(b, g, o - 1).start()
        for o in range(ZN):
            for t in range(TILES):
                po[(g * ZN + o) * TILES + t] = partial_sum(rem(z + ZSHIFT[o], ZN), h, t)
            if o == 0:
                cx_copy(b, g, ZN - 1).start()


    def rs_copy(b, g, side, t):
        i = (b * GROUPS + g) * 2 + side
        n = 2 if t == 0 else 4
        at_ = pl.ds(i * SPAN + OFF[t], n)
        return pltpu.make_async_remote_copy(
            src_ref=sp.at[at_], dst_ref=rp.at[at_], send_sem=rs_s.at[i * 4 + t], recv_sem=rs_r.at[i * 4 + t],
            device_id=(row, zcol(1 if side == 0 else 7)), device_id_type=MESH,
        )

    def chip_sum(b, g, o, t):
        return po[(g * ZN + o) * TILES + t] + cx[((b * GROUPS + g) * ZN + o) * TILES + t]

    def reduce_step(b, g, t):
        for o in (0,) if t == 0 else (2 * t - 1, 2 * t):
            cx_copy(b, g, o).wait_recv()
        for side in (0, 1):
            base = ((b * GROUPS + g) * 2 + side) * SPAN
            o = 0 if t == 0 else 2 * t - 1 + side
            if t:
                rs_copy(b, g, side, t - 1).wait_recv()
            if t == 0:
                for n in range(2):
                    sp[base + n] = chip_sum(b, g, 0, 2 * side + n)
            else:
                for n in range(4):
                    val = chip_sum(b, g, o, n)
                    if t > 1:
                        val = val + rp[base + OFF[t - 1] + n]
                    elif n // 2 == side:
                        val = val + rp[base + n - 2 * side]
                    sp[base + OFF[t] + n] = val
            go(rs_copy(b, g, side, t))

    def reduce_last(b, g):
        cx_copy(b, g, ZN - 1).wait_recv()
        for side in (0, 1):
            rs_copy(b, g, side, 3).wait_recv()
        base = (b * GROUPS + g) * 2 * SPAN
        for n in range(TILES):
            val = xg[tile0(0, g, row) + n] + chip_sum(b, g, ZN - 1, n)
            val = val + rp[base + OFF[3] + n] + rp[base + SPAN + OFF[3] + n]
            if b + 1 < ITERS:
                xg[tile0(b + 1, g, row) + n] = val
            else:
                fx[g * TILES + n] = val
        if b + 1 < ITERS:
            gather_own(b + 1, g)
            split(b + 1, g, row)

    plan = Schedule()

    def plan_gather(b, g, t0, own):
        if b == 0:
            plan.add(own, lambda: (gather_own(b, g)))
            plan.add(own, lambda: split(b, g, row))
        plan.add(t0 + 3.0, lambda: first_full(b, g, 0))
        plan.add(t0 + 3.2, lambda: first_full(b, g, 1))
        plan.add(t0 + 3.5, lambda: line_full(b, g, 0, 0))
        plan.add(t0 + 3.7, lambda: line_full(b, g, 0, 1))
        plan.add(t0 + 4.8, lambda: first_far(b, g))
        plan.add(t0 + 5.5, lambda: line_full(b, g, 1, 0))
        plan.add(t0 + 5.7, lambda: line_full(b, g, 1, 1))
        plan.add(t0 + 6.5, lambda: line_full(b, g, 2, 0))
        plan.add(t0 + 6.7, lambda: line_full(b, g, 2, 1))
        plan.add(t0 + 7.0, lambda: line_far(b, g, 0))
        plan.add(t0 + 8.5, lambda: line_full(b, g, 3, 0))
        plan.add(t0 + 8.7, lambda: line_full(b, g, 3, 1))
        plan.add(t0 + 9.0, lambda: line_far(b, g, 1))
        plan.add(t0 + 9.7, lambda: line_far(b, g, 2))
        plan.add(t0 + 10.7, lambda: line_far(b, g, 3))

    def plan_products(b, g, t0, step):
        for piece in range(PIECES):
            plan.add(t0 + piece * step, lambda piece=piece: products(g, piece))
        plan.add(t0 + PIECES * step, lambda: sums(b, g))

    def plan_reduce(b, g, t0):
        for t, when in enumerate((1.0, 3.5, 6.5, 9.5)):
            plan.add(t0 + when, lambda t=t: reduce_step(b, g, t))
        plan.add(t0 + 12.5, lambda: reduce_last(b, g))

    for part in range(2):
        for n in range(4):
            plan.add(2.0 + 4.2 * part + 0.9 * n, lambda part=part, n=n: sort_blocks(part, n))
        plan.add(5.6 + 4.2 * part, lambda part=part: pack_blocks(part))
    plan_gather(0, 0, 0.0, 0.0)
    plan_gather(0, 1, 10.5, 3.3)
    plan_products(0, 0, 11.5, 0.5)
    plan_reduce(0, 0, 16.5)
    plan_products(0, 1, 22.5, 0.5)
    plan_reduce(0, 1, 28.0)
    plan_gather(1, 0, 29.0, 29.0)
    plan_products(1, 0, 41.0, 0.5)
    plan_reduce(1, 0, 46.0)
    plan_gather(1, 1, 41.0, 41.0)
    plan_products(1, 1, 53.0, 0.5)
    plan_reduce(1, 1, 58.0)
    plan.run()

    for j in range(TILES):
        first, second = fx[j], fx[TILES + j]
        out_ref[2 * j] = jnp.where(low, first, pltpu.roll(second, 64, 1))
        out_ref[2 * j + 1] = jnp.where(low, pltpu.roll(first, 64, 1), second)

    for copy in pending:
        copy.wait_send()
    for g in range(GROUPS):
        for o in range(ZN):
            cx_copy(ITERS - 1, g, o).wait_send()


def tables(row_index, col_index, live_count):
    slots = jnp.arange(SLOTS, dtype=jnp.int32)
    rows = jnp.where(slots < live_count[0], row_index, 128)
    key = rows * SLOTS + slots
    rank = jnp.sum((key[None, :] < key[:, None]).astype(jnp.int32), axis=1)
    packed = rows * 128 + col_index
    ordered = jnp.sum(jnp.where(rank[None, :] == slots[:, None], packed[None, :], 0), axis=1)
    rows_in, cols_in = ordered // 128, ordered % 128
    parity = rows_in % 2
    pair = rows_in // 2
    before = jnp.concatenate([jnp.full((1,), -1, jnp.int32), pair[:-1]])
    pairs = jnp.arange(64, dtype=jnp.int32)
    same = pair[None, :] == pairs[:, None]
    upto = jnp.sum((pair[None, :] <= pairs[:, None]).astype(jnp.int32), axis=1)
    ints = jnp.concatenate([(cols_in // 2) * 2 + (cols_in + parity) % 2, jnp.maximum(upto - 1, 0)])
    floats = jnp.concatenate(
        [(pair == before).astype(jnp.float32), parity.astype(jnp.float32), jnp.any(same, axis=1).astype(jnp.float32)]
    )
    return rank[None, :], ints, floats


def body(source, blocks, row_index, col_index, live_count):
    rank, ints, floats = tables(row_index, col_index, live_count)
    f32, bf16 = jnp.float32, jnp.bfloat16
    vmem = pltpu.VMEM
    dma = pltpu.SemaphoreType.DMA
    n = ITERS * GROUPS
    return pl.pallas_call(
        kernel,
        out_shape=jax.ShapeDtypeStruct(source.shape, f32),
        in_specs=[
            pl.BlockSpec(memory_space=pl.ANY),
            pl.BlockSpec(memory_space=pl.ANY),
            pl.BlockSpec(memory_space=vmem),
            pl.BlockSpec(memory_space=pltpu.SMEM),
            pl.BlockSpec(memory_space=pltpu.SMEM),
        ],
        out_specs=pl.BlockSpec(memory_space=vmem),
        scratch_shapes=[
            vmem((ITERS * 128, 64, 128), f32),
            vmem((128, 128, 128), bf16),
            vmem((128, 128, 128), bf16),
            vmem((SLOTS, 128, 128), bf16),
            vmem((SLOTS // 2 * 128, 128), f32),
            vmem((SLOTS, 64, 128), f32),
            vmem((64, 64, SLOTS), f32),
            vmem((SLOTS, SLOTS), bf16),
            vmem((GROUPS * ZN * TILES, 64, 128), f32),
            vmem((GROUPS * ZN * TILES, 64, 128), f32),
            vmem((n * ZN * TILES, 64, 128), f32),
            vmem((n * 2 * SPAN, 64, 128), f32),
            vmem((n * 2 * SPAN, 64, 128), f32),
            vmem((GROUPS * TILES, 64, 128), f32),
            vmem((8, 64, 128), f32),
            dma((n * 20,)),
            dma((n * 20,)),
            dma((n * ZN,)),
            dma((n * ZN,)),
            dma((n * 8,)),
            dma((n * 8,)),
            dma((4,)),
            dma,
        ],
        compiler_params=pltpu.CompilerParams(collective_id=0, has_side_effects=True, vmem_limit_bytes=62 << 20),
        name="bounces",
    )(source, jnp.transpose(blocks, (1, 2, 0)), rank, ints, floats)


def solution(mesh):
    specs = (P(("row", "col"), None, None),) * 2 + (P(("row", "col")),) * 3
    return jax.shard_map(body, mesh=mesh, in_specs=specs, out_specs=specs[0], check_vma=False)
```

time: 518 us -> 164 us (0.32)
  waiting for transfers between devices: 354 us -> 0 us
  Pallas kernels: 0 us -> 157 us
  other arithmetic: 82.4 us -> 2.53 us
  local copies, waits for them, and re-layouts: 36.6 us -> 1.68 us
  matrix products: 29.3 us -> 0 us
  between operations: 13.8 us -> 0.69 us
    psum x2 -> x0, waiting for transfers between devices: 243 us -> none  [body(): whole = lax.psum(partial_value, 'col')]
    pallas_call x0 -> x1, Pallas kernels: none -> 157 us  [body(): pl.pallas_call(kernel, out_shape=jax.ShapeDtypeStruct(source.shape, f32),...]
    all_gather x2 -> x0, waiting for transfers between devices: 110 us -> none  [body(): gathered = lax.all_gather(field, 'row', axis=0, tiled=True)]
    scatter-add x2 -> x0, other arithmetic: 79 us -> none  [local_transfer(): summed = jax.ops.segment_sum(products, row_ids, num_segments=group_rows + 1)]
    dot_general x2 -> x0, matrix products: 29.3 us -> none  [local_transfer(): jnp.einsum('nij,njl->nil', blocks, picked, precision=lax.Precision.HIGHEST)]
    gather x2 -> x0, local copies, waits for them, and re-layouts: 13 us -> none  [local_transfer(): picked = jnp.take(gathered, col_index, axis=0)]
    slice x2 -> x0, local copies, waits for them, and re-layouts: 9.51 us -> none  [local_transfer(): return summed[:group_rows]]
    unnamed x7 -> x3, local copies, waits for them, and re-layouts: 9.17 us -> 1.68 us
  transfers between devices with their start and end apart: 4 -> 0, of which waited for: 4 -> 0; matrix products, arithmetic and copies ran while one was open for 2% -> 0% of each run, Pallas kernels for 0% -> 0%
where the time goes in v1:
time: 164 us; the launch traced here: 162 us
  Pallas kernels  157 us (96%)
  other arithmetic  2.53 us (2%)
  local copies, waits for them, and re-layouts  1.68 us (1%)
    pallas_call x1, Pallas kernels, body(): pl.pallas_call(kernel, out_shape=jax.ShapeDtypeStruct(source.shape, f32),...  157 us

profile of v1, /device:TPU:1, one launch (start us, length us, event | category | flops | bytes accessed | tf_op | source)
XLA Modules:
  0.0 161.9 jit_solution(367108574598263224)
XLA Ops:
  0.7 0.7 multiply_add_fusion
  1.4 0.2 convert_reduce_fusion
  1.5 0.0 copy-start
  1.5 0.1 select_reduce_fusion
  1.7 0.1 fusion
  1.8 0.1 convert_reduce_fusion.1
  1.9 0.1 compare_convert_fusion
  2.0 0.6 pad_add_fusion.mi
  2.6 0.6 pad_maximum_fusion.mf
  3.2 0.0 copy-done
  3.2 157.0 %bounces.1 = f32[8,64,128]{2,1,0:T(8,128)} custom-call(f32[8,64,128]{2,1,0:T(8,128)} %src_hbm.1, f32[64,64,256]{2,1,0:T(8,128)} %bitcast.5, s32[1,256]{1,0:T(1,128)} %bitcast.7, s32[320]{0:T(512)} %pad_add_fusion.mi, f32[576]{0:T(1024)} %pad_maximum_fusion.mf), custom_call_target="tpu_custom_call" | custom-call | tf_op jit(solution)/shard_map/bounces/pallas_call | solution.py:370
  160.2 1.7 %copy.8 = f32[8,64,128]{2,1,0:T(8,128)} copy(f32[8,64,128]{2,1,0:T(8,128)} %bounces.1) | data formatting | bytes 524288
  (4 shorter events, 0.1 us)
Async XLA Ops:
  1.5 1.7 %copy-start = (s32[256]{0:T(256)}, s32[256]{0:T(256)S(1)}, u32[]{:S(2)}) copy-start(s32[256]{0:T(256)S(1)} %convert_reduce_fusion) | copy-start | bytes 3076

commit v2 on v1

v2 whole, which is shorter than its diff:
```python
import jax
import jax.numpy as jnp
from jax import lax
from jax.experimental import pallas as pl
from jax.experimental.pallas import tpu as pltpu
from jax.sharding import PartitionSpec as P

MESH = pl.DeviceIdType.MESH
ITERS = 2
GROUPS = 2
TILES = 4
SLOTS = 256
ROWS = 16
ZN = 8
ZSHIFT = (4, 3, 5, 2, 6, 1, 7, 0)
PIECES = 8
LINES = (0, 3, 1, 2)
SPAN = 14


def rem(a, n):
    return lax.rem(a, n)


ORDER = (
    16, 0, 1, 2, 3, 4, 5, 6, 17, 18, 7, 23, 24, 8, 19, 20, 9, 25, 26, 10, 11, 12, 21, 30, 13, 22, 27, 14, 32, 33, 15,
    39, 40, 28, 29, 31, 34, 35, 38, 36, 37, 72, 41, 44, 42, 43, 45, 46, 47, 73, 74, 48, 79, 80, 49, 75, 76, 50, 81,
    82, 51, 52, 77, 86, 53, 78, 83, 54, 55, 56, 88, 89, 95, 96, 84, 85, 87, 57, 58, 90, 59, 60, 91, 94, 92, 93, 97,
    100, 98, 99, 61, 101, 62, 102, 63, 103, 64, 104, 105, 65, 106, 66, 107, 67, 108, 68, 109, 110, 111, 112, 69, 70,
    113, 114, 115, 116, 71, 117, 118, 119, 120, 128, 129, 121, 134, 135, 122, 130, 131, 123, 136, 137, 124, 132, 141,
    125, 133, 138, 126, 143, 144, 150, 151, 139, 140, 142, 145, 146, 149, 127, 147, 148, 152, 155, 153, 154, 156, 184,
    183, 190, 189, 186, 185, 192, 191, 157, 158, 188, 199, 159, 187, 198, 160, 193, 196, 161, 205, 206, 162, 197, 200,
    163, 194, 195, 164, 202, 203, 201, 165, 166, 167, 204, 207, 210, 209, 168, 169, 208, 170, 171, 212, 211, 213, 214,
    215, 216, 172, 217, 173, 218, 174, 219, 175, 220, 221, 222, 176, 177, 223, 224, 178, 225, 226, 179, 180, 181, 227,
    228, 229, 230, 182, 231, 232, 233, 234, 235, 236, 237,
)


def kernel(
    src_hbm, blk_hbm, mi, mf, out_ref,
    xg, xs0, xs1, a_ref, wide, c_ref, raw, po, px, cx, rp, sp, fx, srcv,
    ag_s, ag_r, cx_s, cx_r, rs_s, rs_r, blk_sem, src_sem,
):
    xs = (xs0, xs1)
    row, col = lax.axis_index("row"), lax.axis_index("col")
    y, x = row // 4, rem(row, 4)
    z, h = col // 2, rem(col, 2)

    def at(i, j):
        return rem(y + i * h + j * (1 - h), 4) * 4 + rem(x + i * (1 - h) + j * h, 4)

    def zcol(d):
        return rem(z + d, ZN) * 2 + h

    partner = z * 2 + (1 - h)

    blk_copies = [
        pltpu.make_async_copy(blk_hbm.at[:, pl.ds(8 * n, 8)], raw.at[:, pl.ds(8 * n, 8)], blk_sem.at[n]) for n in range(4)
    ]
    src_copy = pltpu.make_async_copy(src_hbm, srcv, src_sem)
    src_copy.start()
    for copy in blk_copies:
        copy.start()

    barrier = pltpu.get_barrier_semaphore()
    peers = [(at(1, 0), col), (at(3, 0), col), (at(0, 1), col), (at(0, 3), col)]
    peers += [(row, zcol(1)), (row, zcol(7)), (row, partner)]
    for peer in peers:
        pl.semaphore_signal(barrier, inc=1, device_id=peer, device_id_type=MESH)

    lane = lax.broadcasted_iota(jnp.int32, (64, 128), 1)
    low = lane < 64
    half = jnp.where(lax.broadcasted_iota(jnp.int32, (8, 128), 1) < 64, 1.0, 0.0).astype(jnp.float32)
    flip = 1.0 - 2.0 * half

    src_copy.wait()
    for j in range(TILES):
        even, odd = srcv[2 * j], srcv[2 * j + 1]
        xg[row * 8 + j] = jnp.where(low, even, pltpu.roll(odd, 64, 1))
        xg[row * 8 + TILES + j] = jnp.where(low, pltpu.roll(even, 64, 1), odd)

    pl.semaphore_wait(barrier, len(peers))


    def tile0(b, g, r):
        return b * 128 + r * 8 + g * TILES

    def ag(b, g, k, r, part, dest):
        ref = xg.at[pl.ds(tile0(b, g, r) + 2 * part, 2)]
        i = (b * GROUPS + g) * 30 + k
        return pltpu.make_async_remote_copy(
            src_ref=ref, dst_ref=ref, send_sem=ag_s.at[i], recv_sem=ag_r.at[i], device_id=(dest, col), device_id_type=MESH
        )

    pending = []

    def go(copy):
        copy.start()
        pending.append(copy)

    def split(b, g, r, t0=0, n=TILES):
        for t in range(t0, t0 + n):
            tile = xg[tile0(b, g, r) + t]
            for v, val in enumerate((tile, pltpu.roll(tile, 64, 1))):
                hi = val.astype(jnp.bfloat16)
                lo = (val - hi.astype(jnp.float32)).astype(jnp.bfloat16)
                at_ = (r * TILES + t) * 2 + v
                xs[g][at_, pl.ds(0, 64), :] = hi
                xs[g][at_, pl.ds(64, 64), :] = lo

    ahead, back = (at(1, 0), at(3, 0)), (at(0, 1), at(0, 3))

    def both_ways(b, g, k, r, part, ring):
        near, far = (ring[0], ring[1]) if part == 0 else (ring[1], ring[0])
        go(ag(b, g, k + part, r, part, near))
        go(ag(b, g, k + 3 - part, r, part, far))

    def gather_own(b, g):
        for k, ring in ((0, ahead), (6, back)):
            go(ag(b, g, k, row, 0, ring[0]))
            go(ag(b, g, k + 1, row, 1, ring[1]))
        for k, ring in ((0, ahead), (6, back)):
            go(ag(b, g, k + 2, row, 1, ring[0]))
            go(ag(b, g, k + 3, row, 0, ring[1]))

    def first(b, g, k):
        r = (at(3, 0), at(1, 0), at(3, 0), at(1, 0), at(2, 0), at(2, 0))[k]
        part = (0, 1, 1, 0, 0, 1)[k]
        ag(b, g, k, r, part, row).wait_recv()
        if k < 2:
            go(ag(b, g, 4 + k, r, part, ahead[k]))
        both_ways(b, g, 6 + 6 * (1, 2, 1, 2, 3, 3)[k], r, part, back)
        split(b, g, r, 2 * part, 2)

    def second(b, g, li, k):
        r = at(LINES[li], (3, 1, 3, 1, 2, 2)[k])
        part = (0, 1, 1, 0, 0, 1)[k]
        ag(b, g, 6 + 6 * li + k, r, part, row).wait_recv()
        if k < 2:
            go(ag(b, g, 10 + 6 * li + k, r, part, back[k]))
        split(b, g, r, 2 * part, 2)


    def turn_blocks(n):
        if n % 2 == 0:
            blk_copies[n // 2].wait()
        for i in range(4 * n, 4 * n + 4):
            pair = jnp.concatenate([raw[0, i], raw[1, i]], axis=0)
            wide[pl.ds(i, SLOTS, stride=32), :] = jnp.transpose(pair, (1, 0))

    def pack_blocks(n):
        def one(it, carry):
            for u in range(4):
                s = it * 4 + u
                val = wide[pl.ds(pl.multiple_of(s * 32, 32), 32), :]
                turned = pltpu.roll(val, 64, 1)
                low32 = low[:32]
                both = jnp.concatenate([jnp.where(low32, val, turned), jnp.where(low32, turned, val)], axis=0)
                hi = both.astype(jnp.bfloat16)
                a_ref[s, pl.ds(0, 64), :] = hi
                a_ref[s, pl.ds(64, 64), :] = (both - hi.astype(jnp.float32)).astype(jnp.bfloat16)
            return carry

        lax.fori_loop(8 * n, 8 * n + 8, one, 0)


    def products(g, piece):
        start = piece * (SLOTS // PIECES)

        acc = c_ref[start - 1] if piece else jnp.zeros((64, 128), jnp.float32)
        slots = range(start, start + SLOTS // PIECES)
        found = [jnp.dot(a_ref[mi[SLOTS + 64 + p]], xs[g][mi[p]], preferred_element_type=jnp.float32) for p in slots]
        for p, both in zip(slots, found):
            mask = half + mf[SLOTS + p] * flip
            both = ((both[:64] + both[64:]).reshape(8, 8, 128) * mask[None]).reshape(64, 128)
            acc = acc * mf[p] + both
            c_ref[p] = acc

    def partial_sum(zc, core, t):
        q = (zc * 2 + core) * TILES + t
        return c_ref[mi[SLOTS + q]] * mf[2 * SLOTS + q]

    def cx_copy(b, g, o):
        i = (b * GROUPS + g) * ZN + o
        return pltpu.make_async_remote_copy(
            src_ref=px.at[pl.ds((g * ZN + o) * TILES, TILES)], dst_ref=cx.at[pl.ds(i * TILES, TILES)],
            send_sem=cx_s.at[i], recv_sem=cx_r.at[i], device_id=(row, partner), device_id_type=MESH,
        )

    def sums_out(b, g):
        if b:
            for o in range(ZN):
                cx_copy(b - 1, g, o).wait_send()
        for o in range(ZN):
            for t in range(TILES):
                px[(g * ZN + o) * TILES + t] = partial_sum(rem(z + ZSHIFT[o], ZN), 1 - h, t)
            if o:
                cx_copy(b, g, o - 1).start()

    def sums_own(b, g):
        for o in range(ZN):
            for t in range(TILES):
                po[(g * ZN + o) * TILES + t] = partial_sum(rem(z + ZSHIFT[o], ZN), h, t)
            if o == 0:
                cx_copy(b, g, ZN - 1).start()


    def rs_copy(b, g, side, m):
        i = (b * GROUPS + g) * 2 + side
        at_ = pl.ds(i * SPAN + m, 1)
        return pltpu.make_async_remote_copy(
            src_ref=sp.at[at_], dst_ref=rp.at[at_], send_sem=rs_s.at[i * SPAN + m], recv_sem=rs_r.at[i * SPAN + m],
            device_id=(row, zcol(1 if side == 0 else 7)), device_id_type=MESH,
        )

    def chip_sum(b, g, o, t):
        return po[(g * ZN + o) * TILES + t] + cx[((b * GROUPS + g) * ZN + o) * TILES + t]

    def reduce_step(b, g, m):
        q, n = m // 2, m % 2
        t, chain = (q + 1) // 2, q % 2
        if n == 0:
            for o in (2 * t - 1, 2 * t) if chain else (0,) if t == 0 else ():
                cx_copy(b, g, o).wait_recv()
        for side in (0, 1):
            base = ((b * GROUPS + g) * 2 + side) * SPAN
            o = 0 if t == 0 else 2 * t - 1 + side
            val = chip_sum(b, g, o, 2 * ((side + chain) % 2) + n)
            if q > 1:
                rs_copy(b, g, side, m - 4).wait_recv()
                val = val + rp[base + m - 4]
            sp[base + m] = val
        for side in (0, 1):
            go(rs_copy(b, g, side, m))

    def reduce_last(b, g):
        cx_copy(b, g, ZN - 1).wait_recv()
        for side in (0, 1):
            for m in range(10, 14):
                rs_copy(b, g, side, m).wait_recv()
        base = (b * GROUPS + g) * 2 * SPAN
        for n in range(TILES):
            val = xg[tile0(0, g, row) + n] + chip_sum(b, g, ZN - 1, n)
            for side in (0, 1):
                m = 12 if n // 2 == side else 10
                val = val + rp[base + side * SPAN + m + n % 2]
            if b + 1 < ITERS:
                xg[tile0(b + 1, g, row) + n] = val
            else:
                fx[g * TILES + n] = val
        if b + 1 < ITERS:
            gather_own(b + 1, g)
            split(b + 1, g, row)

    tasks = []
    for n in range(8):
        tasks.append(lambda n=n: turn_blocks(n))
    for n in range(8):
        tasks.append(lambda n=n: pack_blocks(n))
    for b in range(ITERS):
        for g in range(GROUPS):
            if b == 0:
                tasks.append(lambda b=b, g=g: (gather_own(b, g), split(b, g, row)))
            for k in range(6):
                tasks.append(lambda b=b, g=g, k=k: first(b, g, k))
            for li in range(4):
                for k in range(4):
                    tasks.append(lambda b=b, g=g, li=li, k=k: second(b, g, li, k))
            for li in range(4):
                for k in range(4, 6):
                    tasks.append(lambda b=b, g=g, li=li, k=k: second(b, g, li, k))
            for piece in range(PIECES):
                tasks.append(lambda g=g, piece=piece: products(g, piece))
            tasks.append(lambda b=b, g=g: sums_out(b, g))
            tasks.append(lambda b=b, g=g: sums_own(b, g))
            for m in range(14):
                tasks.append(lambda b=b, g=g, m=m: reduce_step(b, g, m))
            tasks.append(lambda b=b, g=g: reduce_last(b, g))
    for n in ORDER:
        tasks[n]()

    for j in range(TILES):
        first, second = fx[j], fx[TILES + j]
        out_ref[2 * j] = jnp.where(low, first, pltpu.roll(second, 64, 1))
        out_ref[2 * j + 1] = jnp.where(low, pltpu.roll(first, 64, 1), second)

    for copy in pending:
        copy.wait_send()
    for g in range(GROUPS):
        for o in range(ZN):
            cx_copy(ITERS - 1, g, o).wait_send()


def tables(row_index, col_index, live_count):
    slots = jnp.arange(SLOTS, dtype=jnp.int32)
    rows = jnp.where(slots < live_count[0], row_index, 128)
    key = rows * SLOTS + slots
    rank = jnp.sum((key[None, :] < key[:, None]).astype(jnp.int32), axis=1)
    packed = key * 128 + col_index
    ordered = jnp.sum(jnp.where(rank[None, :] == slots[:, None], packed[None, :], 0), axis=1)
    keys_in, cols_in = ordered // 128, ordered % 128
    rows_in, slots_in = keys_in // SLOTS, keys_in % SLOTS
    parity = rows_in % 2
    pair = rows_in // 2
    before = jnp.concatenate([jnp.full((1,), -1, jnp.int32), pair[:-1]])
    pairs = jnp.arange(64, dtype=jnp.int32)
    same = pair[None, :] == pairs[:, None]
    upto = jnp.sum((pair[None, :] <= pairs[:, None]).astype(jnp.int32), axis=1)
    ints = jnp.concatenate([(cols_in // 2) * 2 + (cols_in + parity) % 2, jnp.maximum(upto - 1, 0), slots_in])
    floats = jnp.concatenate(
        [(pair == before).astype(jnp.float32), parity.astype(jnp.float32), jnp.any(same, axis=1).astype(jnp.float32)]
    )
    return ints, floats


def body(source, blocks, row_index, col_index, live_count):
    ints, floats = tables(row_index, col_index, live_count)
    f32, bf16 = jnp.float32, jnp.bfloat16
    vmem = pltpu.VMEM
    dma = pltpu.SemaphoreType.DMA
    n = ITERS * GROUPS
    return pl.pallas_call(
        kernel,
        out_shape=jax.ShapeDtypeStruct(source.shape, f32),
        in_specs=[
            pl.BlockSpec(memory_space=pl.ANY),
            pl.BlockSpec(memory_space=pl.ANY),
            pl.BlockSpec(memory_space=pltpu.SMEM),
            pl.BlockSpec(memory_space=pltpu.SMEM),
        ],
        out_specs=pl.BlockSpec(memory_space=vmem),
        scratch_shapes=[
            vmem((ITERS * 128, 64, 128), f32),
            vmem((128, 128, 128), bf16),
            vmem((128, 128, 128), bf16),
            vmem((SLOTS, 128, 128), bf16),
            vmem((SLOTS * 32, 128), f32),
            vmem((SLOTS, 64, 128), f32),
            vmem((2, 32, 64, SLOTS), f32),
            vmem((GROUPS * ZN * TILES, 64, 128), f32),
            vmem((GROUPS * ZN * TILES, 64, 128), f32),
            vmem((n * ZN * TILES, 64, 128), f32),
            vmem((n * 2 * SPAN, 64, 128), f32),
            vmem((n * 2 * SPAN, 64, 128), f32),
            vmem((GROUPS * TILES, 64, 128), f32),
            vmem((8, 64, 128), f32),
            dma((n * 30,)),
            dma((n * 30,)),
            dma((n * ZN,)),
            dma((n * ZN,)),
            dma((n * 2 * SPAN,)),
            dma((n * 2 * SPAN,)),
            dma((4,)),
            dma,
        ],
        compiler_params=pltpu.CompilerParams(collective_id=0, has_side_effects=True, vmem_limit_bytes=62 << 20),
        name="bounces",
    )(source, jnp.transpose(blocks, (1, 2, 0)).reshape(2, 32, 64, SLOTS), ints, floats)


def solution(mesh):
    specs = (P(("row", "col"), None, None),) * 2 + (P(("row", "col")),) * 3
    return jax.shard_map(body, mesh=mesh, in_specs=specs, out_specs=specs[0], check_vma=False)
```

time: 164 us -> 114 us (0.70)
  Pallas kernels: 157 us -> 107 us
    pallas_call x1, Pallas kernels: 157 us -> 107 us  [body(): pl.pallas_call(kernel, out_shape=jax.ShapeDtypeStruct(source.shape, f32),...]
where the time goes in v2:
time: 114 us; the launch traced here: 112 us
  Pallas kernels  107 us (94%)
  other arithmetic  2.64 us (2%)
  local copies, waits for them, and re-layouts  1.67 us (1%)
    pallas_call x1, Pallas kernels, body(): pl.pallas_call(kernel, out_shape=jax.ShapeDtypeStruct(source.shape, f32),...  107 us

profile of v2, /device:TPU:1, one launch (start us, length us, event | category | flops | bytes accessed | tf_op | source)
XLA Modules:
  0.0 112.5 jit_solution(15535519964092150337)
XLA Ops:
  0.7 0.7 multiply_add_fusion
  1.4 0.2 convert_reduce_fusion
  1.5 0.1 select_reduce_fusion
  1.7 0.1 fusion
  1.9 0.1 convert_reduce_fusion.1
  2.0 0.1 compare_convert_fusion
  2.0 0.7 pad_add_fusion.mi
  2.7 0.6 pad_maximum_fusion.mf
  3.3 107.5 %bounces.1 = f32[8,64,128]{2,1,0:T(8,128)} custom-call(f32[8,64,128]{2,1,0:T(8,128)} %src_hbm.1, f32[2,32,64,256]{3,2,1,0:T(8,128)} %bitcast.6, s32[576]{0:T(1024)} %pad_add_fusion.mi, f32[576]{0:T(1024)} %pad_maximum_fusion.mf), custom_call_target="tpu_custom_call" | custom-call | tf_op jit(solution)/shard_map/bounces/pallas_call | solution.py:322
  110.8 1.7 %copy.8 = f32[8,64,128]{2,1,0:T(8,128)} copy(f32[8,64,128]{2,1,0:T(8,128)} %bounces.1) | data formatting | bytes 524288
  (5 shorter events, 0.1 us)

commit v3 on v2

--- a/solution.py
+++ b/solution.py
@@ -23,16 +23,16 @@
 
 
 ORDER = (
-    16, 0, 1, 2, 3, 4, 5, 6, 17, 18, 7, 23, 24, 8, 19, 20, 9, 25, 26, 10, 11, 12, 21, 30, 13, 22, 27, 14, 32, 33, 15,
-    39, 40, 28, 29, 31, 34, 35, 38, 36, 37, 72, 41, 44, 42, 43, 45, 46, 47, 73, 74, 48, 79, 80, 49, 75, 76, 50, 81,
-    82, 51, 52, 77, 86, 53, 78, 83, 54, 55, 56, 88, 89, 95, 96, 84, 85, 87, 57, 58, 90, 59, 60, 91, 94, 92, 93, 97,
-    100, 98, 99, 61, 101, 62, 102, 63, 103, 64, 104, 105, 65, 106, 66, 107, 67, 108, 68, 109, 110, 111, 112, 69, 70,
-    113, 114, 115, 116, 71, 117, 118, 119, 120, 128, 129, 121, 134, 135, 122, 130, 131, 123, 136, 137, 124, 132, 141,
-    125, 133, 138, 126, 143, 144, 150, 151, 139, 140, 142, 145, 146, 149, 127, 147, 148, 152, 155, 153, 154, 156, 184,
-    183, 190, 189, 186, 185, 192, 191, 157, 158, 188, 199, 159, 187, 198, 160, 193, 196, 161, 205, 206, 162, 197, 200,
-    163, 194, 195, 164, 202, 203, 201, 165, 166, 167, 204, 207, 210, 209, 168, 169, 208, 170, 171, 212, 211, 213, 214,
-    215, 216, 172, 217, 173, 218, 174, 219, 175, 220, 221, 222, 176, 177, 223, 224, 178, 225, 226, 179, 180, 181, 227,
-    228, 229, 230, 182, 231, 232, 233, 234, 235, 236, 237,
+    16, 0, 1, 2, 3, 4, 5, 17, 18, 6, 23, 24, 7, 19, 20, 8, 9, 25, 26, 10, 21, 30, 11, 22, 27, 12, 32, 33, 13, 14, 39,
+    40, 15, 28, 29, 31, 34, 35, 38, 36, 72, 37, 41, 44, 42, 43, 45, 46, 47, 48, 49, 73, 74, 50, 51, 79, 80, 52, 53,
+    54, 55, 56, 75, 76, 81, 82, 57, 58, 77, 86, 59, 60, 83, 78, 89, 88, 61, 95, 96, 62, 85, 84, 63, 87, 90, 64, 91,
+    94, 65, 97, 92, 66, 93, 100, 67, 99, 98, 68, 101, 102, 103, 104, 69, 105, 106, 107, 70, 108, 109, 110, 111, 112,
+    113, 114, 115, 116, 71, 128, 117, 118, 129, 130, 119, 135, 136, 120, 131, 132, 121, 137, 138, 122, 133, 142, 123,
+    134, 139, 124, 144, 145, 125, 151, 152, 126, 140, 141, 143, 146, 147, 150, 148, 149, 127, 184, 153, 156, 154, 155,
+    157, 158, 159, 160, 161, 185, 186, 162, 163, 191, 192, 164, 165, 166, 167, 168, 187, 188, 193, 194, 169, 170, 189,
+    198, 171, 172, 195, 190, 201, 200, 173, 207, 208, 174, 197, 196, 175, 199, 202, 176, 203, 206, 177, 209, 204, 178,
+    205, 212, 179, 211, 210, 180, 213, 214, 215, 216, 181, 217, 218, 219, 182, 220, 221, 222, 223, 224, 225, 226, 227,
+    228, 183, 229, 230, 231, 232, 233, 234, 235, 236, 237, 238, 239,
 )
 
 
@@ -248,10 +248,6 @@
                 xg[tile0(b + 1, g, row) + n] = val
             else:
                 fx[g * TILES + n] = val
-        if b + 1 < ITERS:
-            gather_own(b + 1, g)
-            split(b + 1, g, row)
-
     tasks = []
     for n in range(8):
         tasks.append(lambda n=n: turn_blocks(n))
@@ -259,8 +255,7 @@
         tasks.append(lambda n=n: pack_blocks(n))
     for b in range(ITERS):
         for g in range(GROUPS):
-            if b == 0:
-                tasks.append(lambda b=b, g=g: (gather_own(b, g), split(b, g, row)))
+            tasks.append(lambda b=b, g=g: (gather_own(b, g), split(b, g, row)))
             for k in range(6):
                 tasks.append(lambda b=b, g=g, k=k: first(b, g, k))
             for li in range(4):

time: 114 us -> 108 us (0.947)
  Pallas kernels: 107 us -> 103 us
    pallas_call x1, Pallas kernels: 107 us -> 103 us  [body(): pl.pallas_call(kernel, out_shape=jax.ShapeDtypeStruct(source.shape, f32),...]
where the time goes in v3:
time: 108 us
  Pallas kernels  103 us (95%)
  other arithmetic  2.64 us (2%)
  local copies, waits for them, and re-layouts  1.67 us (2%)
    pallas_call x1, Pallas kernels, body(): pl.pallas_call(kernel, out_shape=jax.ShapeDtypeStruct(source.shape, f32),...  103 us

profile of v3, /device:TPU:1, one launch (start us, length us, event | category | flops | bytes accessed | tf_op | source)
XLA Modules:
  0.0 107.6 jit_solution(12380852382088618410)
XLA Ops:
  0.7 0.7 multiply_add_fusion
  1.4 0.2 convert_reduce_fusion
  1.5 0.1 select_reduce_fusion
  1.7 0.1 fusion
  1.9 0.1 convert_reduce_fusion.1
  2.0 0.1 compare_convert_fusion
  2.0 0.7 pad_add_fusion.mi
  2.7 0.6 pad_maximum_fusion.mf
  3.3 102.6 %bounces.1 = f32[8,64,128]{2,1,0:T(8,128)} custom-call(f32[8,64,128]{2,1,0:T(8,128)} %src_hbm.1, f32[2,32,64,256]{3,2,1,0:T(8,128)} %bitcast.6, s32[576]{0:T(1024)} %pad_add_fusion.mi, f32[576]{0:T(1024)} %pad_maximum_fusion.mf), custom_call_target="tpu_custom_call" | custom-call | tf_op jit(solution)/shard_map/bounces/pallas_call | solution.py:317
  106.0 1.7 %copy.8 = f32[8,64,128]{2,1,0:T(8,128)} copy(f32[8,64,128]{2,1,0:T(8,128)} %bounces.1) | data formatting | bytes 524288
  (5 shorter events, 0.1 us)
